TPU v7x, 32 devices: a whole 2x2x4 slice. The times are simulated.
32 devices in a mesh: layer: 4 (over y, x), feat: 8 (over z, core).
Axes of the slice: x: 2, y: 2, z: 4, core: 2. Of those that a mesh axis runs over, the one named last changes fastest.
Arguments:
- acts: bfloat16 [4, 256, 8192], P(None, 'layer', 'feat'), may hold values from -6 to 6
- layer_order: int32 [4, 4], P('layer'), may hold values from 0 to 3, each once within a row
- groups: int32 [8192], P('feat'), may hold values from 0 to 63
- group_scale: float32 [4, 64], P('layer'), may hold values from 0.25 to 4
- shrink: float32 [4], P('layer'), may hold values from 0.1 to 0.6
Outputs:
- factor_tiles: float32 [4, 8, 4, 1024, 1024], P('layer', 'feat')
- far_tiles: float32 [4, 8, 512, 1024], P('layer', 'feat')
Inputs may be any that keep to these rules, and one draw needn't show every extreme that they name: Each row of layer_order names every layer once.
All inputs are finite; a program needn't handle non-finite values.
Results may differ from a plain program's by a relative error of at most 0.0003.
Values may be sent and summed in bfloat16 or wider, within the bound.
No kernel may reach another device: no remote copies, remote signals or barrier semaphores. Data moves between devices by JAX's collectives and lax.ppermute only.
A program may use at most 64 MiB of HBM per device.

v0:
```python
import jax
import jax.numpy as jnp
from jax import lax
from jax.sharding import PartitionSpec as P


def shifted(block, axis, distance):
    devices = range(lax.axis_size(axis))
    route = [((i - distance) % len(devices), i) for i in devices]
    return lax.ppermute(block, axis, route)


def product(left, right):
    return lax.dot_general(
        left, right, (((0,), (0,)), ((), ())), preferred_element_type=jnp.float32
    )


def shards(acts, layer_order, groups, group_scale, shrink):
    layers = acts.shape[0]
    pick = (layer_order[0][None, :] == jnp.arange(layers, dtype=jnp.int32)[:, None]).astype(
        jnp.bfloat16
    )
    ordered = jnp.einsum("ds,stc->dtc", pick, acts, preferred_element_type=jnp.float32).astype(
        jnp.bfloat16
    )
    gathered = lax.all_to_all(ordered, "layer", split_axis=0, concat_axis=1, tiled=True)
    panel = gathered[0]
    tokens = panel.shape[0]
    width = panel.shape[1]
    half = lax.axis_size("feat") // 2

    def advance(index, carry):
        moving, stack = carry
        stack = lax.dynamic_update_slice_in_dim(stack, product(panel, moving)[None], index, 0)
        moving = shifted(moving, "feat", -1)
        return (moving, stack)

    start = (panel, jnp.zeros((half, width, width), jnp.float32))
    opposite, grams = lax.fori_loop(0, half, advance, start)
    weight = shrink[0]
    scaled = grams / tokens * (1.0 - weight)
    local_trace = jnp.sum(jnp.diagonal(grams[0]) / tokens)
    mu = lax.psum(local_trace, "feat") / (width * lax.axis_size("feat"))
    members = (
        groups[:, None] == jnp.arange(group_scale.shape[1], dtype=jnp.int32)[None, :]
    ).astype(jnp.float32)
    gains = jnp.dot(members, group_scale[0], precision=lax.Precision.HIGHEST)
    diagonal = weight * mu * gains
    identity = jnp.eye(width, dtype=jnp.float32)
    factor = scaled.at[0].add(diagonal[:, None] * identity)
    lower = lax.axis_index("feat") < half
    rows_half = width // 2
    left = jnp.where(lower, panel[:, :rows_half], opposite[:, rows_half:])
    right = jnp.where(lower, opposite, panel)
    far = product(left, right) / tokens * (1.0 - weight)
    return (factor[None, None], far[None, None])


def solution(mesh):
    placed = (P(None, "layer", "feat"), P("layer", None), P("feat"), P("layer", None), P("layer"))
    return jax.shard_map(
        shards,
        mesh=mesh,
        in_specs=placed,
        out_specs=(P("layer", "feat", None, None, None), P("layer", "feat", None, None)),
        check_vma=False,
    )
```

profile of v0, /device:TPU:0, one launch (start us, length us, event | category | flops | bytes accessed | tf_op | source)
XLA Modules:
  0.0 129.8 jit_solution(15302970972623566115)
XLA Ops:
  0.6 0.0 copy-start
  0.6 1.0 copy-done
  1.7 1.1 convolution_convert_fusion
  2.8 1.0 copy.11
  3.8 5.2 %all-to-all-start = ((bf16[4,64,1024]{2,1,0:T(8,128)(2,1)}), bf16[4,64,1024]{2,1,0:T(8,128)(2,1)S(1)}, u32[]{:S(2)}, u32[]{:S(2)}) async-start(bf16[4,64,1024]{2,1,0:T(8,128)(2,1)} %copy.11), calls=%async_computation | async-start | bytes 1048576 | tf_op jit(solution)/shard_map/all_to_all | solution.py:27
  9.6 1.1 fusion.5
  10.8 6.2 %all-to-all-done = bf16[4,64,1024]{2,1,0:T(8,128)(2,1)S(1)} async-done(((bf16[4,64,1024]{2,1,0:T(8,128)(2,1)}), bf16[4,64,1024]{2,1,0:T(8,128)(2,1)S(1)}, u32[]{:S(2)}, u32[]{:S(2)}) %all-to-all-start) | async-done | bytes 524320 | tf_op jit(solution)/shard_map/all_to_all | solution.py:27
  17.0 40.3 %while.16 = (s32[]{:T(128)}, bf16[256,1024]{1,0:T(8,128)(2,1)S(1)}, f32[4,1024,1024]{2,1,0:T(8,128)}, bf16[256,1024]{1,0:T(8,128)(2,1)S(1)}, s32[]{:T(128)}) while((s32[]{:T(128)}, bf16[256,1024]{1,0:T(8,128)(2,1)S(1)}, f32[4,1024,1024]{2,1,0:T(8,128)}, bf16[256,1024]{1,0:T(8,128)(2,1)S(1)}, s32[]{:T(128)}) %tuple.39), condition=%wide.region_1.0_spmd, body=%wide.region_0.0_spmd.sunk | while | flops 536870912 | bytes 8388721 | solution.py:40
  17.1 2.0 %collective-permute-start = (bf16[256,1024]{1,0:T(8,128)(2,1)S(1)}, bf16[256,1024]{1,0:T(8,128)(2,1)S(1)}, u32[]{:S(2)}, u32[]{:S(2)}) collective-permute-start(bf16[256,1024]{1,0:T(8,128)(2,1)S(1)} %copy.19), channel_id=1, source_target_pairs={{1,0},{2,1},{3,2},{4,3},{5,4},{6,5},{7,6},{0,7},{9,8},{10,9},{11,1... | collective-permute-start | bytes 1572872 | tf_op jit(solution)/shard_map/while/body/eval_jaxpr/ppermute | solution.py:10
  19.1 2.8 %bitcast_dynamic-update-slice_fusion.2 = f32[4,1024,1024]{2,1,0:T(8,128)} fusion(f32[4,1024,1024]{2,1,0:T(8,128)} %get-tuple-element.136, s32[]{:T(128)S(6)} %copy.18, bf16[256,1024]{1,0:T(8,128)(2,1)S(1)} %get-tuple-element.142, bf16[256,1024]{1,0:T(8,128)(2,1)S(1)} %copy.19), kind=kOutput, calls=%fused_computation.1.clone.1 | convolution fusion | flops 536870912 | bytes 5242884 | tf_op jit(solution)/shard_map/while/body/eval_jaxpr/dot_general | solution.py:14
  21.9 3.9 %collective-permute-done = bf16[256,1024]{1,0:T(8,128)(2,1)S(1)} collective-permute-done((bf16[256,1024]{1,0:T(8,128)(2,1)S(1)}, bf16[256,1024]{1,0:T(8,128)(2,1)S(1)}, u32[]{:S(2)}, u32[]{:S(2)}) %collective-permute-start) | collective-permute-done | bytes 524320 | tf_op jit(solution)/shard_map/while/body/eval_jaxpr/ppermute | solution.py:10
  25.8 3.8 %collective-permute-start = (bf16[256,1024]{1,0:T(8,128)(2,1)S(1)}, bf16[256,1024]{1,0:T(8,128)(2,1)S(1)}, u32[]{:S(2)}, u32[]{:S(2)}) collective-permute-start(bf16[256,1024]{1,0:T(8,128)(2,1)S(1)} %copy.19), channel_id=1, source_target_pairs={{1,0},{2,1},{3,2},{4,3},{5,4},{6,5},{7,6},{0,7},{9,8},{10,9},{11,1... | collective-permute-start | bytes 1572872 | tf_op jit(solution)/shard_map/while/body/eval_jaxpr/ppermute | solution.py:10
  29.6 2.8 %bitcast_dynamic-update-slice_fusion.2 = f32[4,1024,1024]{2,1,0:T(8,128)} fusion(f32[4,1024,1024]{2,1,0:T(8,128)} %get-tuple-element.136, s32[]{:T(128)S(6)} %copy.18, bf16[256,1024]{1,0:T(8,128)(2,1)S(1)} %get-tuple-element.142, bf16[256,1024]{1,0:T(8,128)(2,1)S(1)} %copy.19), kind=kOutput, calls=%fused_computation.1.clone.1 | convolution fusion | flops 536870912 | bytes 5242884 | tf_op jit(solution)/shard_map/while/body/eval_jaxpr/dot_general | solution.py:14
  32.4 3.9 %collective-permute-done = bf16[256,1024]{1,0:T(8,128)(2,1)S(1)} collective-permute-done((bf16[256,1024]{1,0:T(8,128)(2,1)S(1)}, bf16[256,1024]{1,0:T(8,128)(2,1)S(1)}, u32[]{:S(2)}, u32[]{:S(2)}) %collective-permute-start) | collective-permute-done | bytes 524320 | tf_op jit(solution)/shard_map/while/body/eval_jaxpr/ppermute | solution.py:10
  36.3 3.8 %collective-permute-start = (bf16[256,1024]{1,0:T(8,128)(2,1)S(1)}, bf16[256,1024]{1,0:T(8,128)(2,1)S(1)}, u32[]{:S(2)}, u32[]{:S(2)}) collective-permute-start(bf16[256,1024]{1,0:T(8,128)(2,1)S(1)} %copy.19), channel_id=1, source_target_pairs={{1,0},{2,1},{3,2},{4,3},{5,4},{6,5},{7,6},{0,7},{9,8},{10,9},{11,1... | collective-permute-start | bytes 1572872 | tf_op jit(solution)/shard_map/while/body/eval_jaxpr/ppermute | solution.py:10
  40.1 2.8 %bitcast_dynamic-update-slice_fusion.2 = f32[4,1024,1024]{2,1,0:T(8,128)} fusion(f32[4,1024,1024]{2,1,0:T(8,128)} %get-tuple-element.136, s32[]{:T(128)S(6)} %copy.18, bf16[256,1024]{1,0:T(8,128)(2,1)S(1)} %get-tuple-element.142, bf16[256,1024]{1,0:T(8,128)(2,1)S(1)} %copy.19), kind=kOutput, calls=%fused_computation.1.clone.1 | convolution fusion | flops 536870912 | bytes 5242884 | tf_op jit(solution)/shard_map/while/body/eval_jaxpr/dot_general | solution.py:14
  42.9 3.9 %collective-permute-done = bf16[256,1024]{1,0:T(8,128)(2,1)S(1)} collective-permute-done((bf16[256,1024]{1,0:T(8,128)(2,1)S(1)}, bf16[256,1024]{1,0:T(8,128)(2,1)S(1)}, u32[]{:S(2)}, u32[]{:S(2)}) %collective-permute-start) | collective-permute-done | bytes 524320 | tf_op jit(solution)/shard_map/while/body/eval_jaxpr/ppermute | solution.py:10
  46.8 3.8 %collective-permute-start = (bf16[256,1024]{1,0:T(8,128)(2,1)S(1)}, bf16[256,1024]{1,0:T(8,128)(2,1)S(1)}, u32[]{:S(2)}, u32[]{:S(2)}) collective-permute-start(bf16[256,1024]{1,0:T(8,128)(2,1)S(1)} %copy.19), channel_id=1, source_target_pairs={{1,0},{2,1},{3,2},{4,3},{5,4},{6,5},{7,6},{0,7},{9,8},{10,9},{11,1... | collective-permute-start | bytes 1572872 | tf_op jit(solution)/shard_map/while/body/eval_jaxpr/ppermute | solution.py:10
  50.6 2.8 %bitcast_dynamic-update-slice_fusion.2 = f32[4,1024,1024]{2,1,0:T(8,128)} fusion(f32[4,1024,1024]{2,1,0:T(8,128)} %get-tuple-element.136, s32[]{:T(128)S(6)} %copy.18, bf16[256,1024]{1,0:T(8,128)(2,1)S(1)} %get-tuple-element.142, bf16[256,1024]{1,0:T(8,128)(2,1)S(1)} %copy.19), kind=kOutput, calls=%fused_computation.1.clone.1 | convolution fusion | flops 536870912 | bytes 5242884 | tf_op jit(solution)/shard_map/while/body/eval_jaxpr/dot_general | solution.py:14
  53.3 3.9 %collective-permute-done = bf16[256,1024]{1,0:T(8,128)(2,1)S(1)} collective-permute-done((bf16[256,1024]{1,0:T(8,128)(2,1)S(1)}, bf16[256,1024]{1,0:T(8,128)(2,1)S(1)}, u32[]{:S(2)}, u32[]{:S(2)}) %collective-permute-start) | collective-permute-done | bytes 524320 | tf_op jit(solution)/shard_map/while/body/eval_jaxpr/ppermute | solution.py:10
  57.3 4.7 %slice_bitcast_fusion = f32[1024,1024]{1,0:T(8,128)} fusion(f32[4,1024,1024]{2,1,0:T(8,128)} %get-tuple-element.94), kind=kLoop, calls=%fused_computation.6 | loop fusion | bytes 8388608 | tf_op jit(solution)/shard_map/squeeze | solution.py:43
  62.0 17.3 %gather_fusion = f32[1024]{0:T(1024)S(1)} fusion(f32[1024,1024]{1,0:T(8,128)} %slice_bitcast_fusion, s32[1024]{0:T(1024)S(1)} %bitcast.36), kind=kCustom, calls=%fused_computation | custom fusion | bytes 16384 | tf_op jit(solution)/shard_map/jit(diagonal)/cond/branch_0_fun/gather | solution.py:43
  79.3 0.6 multiply_reduce_fusion
  79.9 12.2 %broadcast_multiply_fusion = f32[4,1024,1024]{2,1,0:T(8,128)} fusion(f32[4,1024,1024]{2,1,0:T(8,128)} %get-tuple-element.94, f32[]{:T(128)S(6)} %mul.31), kind=kLoop, calls=%fused_computation.2 | loop fusion | flops 4194304 | bytes 33554436 | tf_op jit(solution)/shard_map/mul | solution.py:42
  92.1 12.4 %fusion.15 = f32[1,1,4,1024,1024]{4,3,2,1,0:T(8,128)} fusion(f32[4,1024,1024]{2,1,0:T(8,128)} %get-tuple-element.94, f32[]{:T(128)S(6)} %mul.31), kind=kLoop, calls=%fused_computation.26 | loop fusion | flops 4194304 | bytes 33554436 | tf_op jit(solution)/shard_map/broadcast_in_dim | solution.py:57
  104.5 18.0 %psum.7 = f32[]{:T(128)} all-reduce(f32[]{:T(128)} %multiply_reduce_fusion), channel_id=1, replica_groups=mesh['layer'=4,'feat'=8] {'feat'}, use_global_device_ids=true, to_apply=%region_3.4 | all-reduce | flops 1 | bytes 8 | tf_op jit(solution)/shard_map/psum | solution.py:44
  122.4 1.8 %multiply_bitcast_fusion = f32[1,1,512,1024]{3,2,1,0:T(8,128)} fusion(f32[]{:T(128)S(6)} %mul.31, bf16[256,1024]{1,0:T(8,128)(2,1)S(1)} %get-tuple-element.95, bf16[256,1024]{1,0:T(8,128)(2,1)S(1)} %get-tuple-element.145, pred[]{:T(512)S(6)} %lt.17), kind=kOutput, calls=%fused_computation.8 | convolution fusion | flops 269352960 | bytes 3671552 | tf_op jit(solution)/shard_map/dot_general | solution.py:14
  124.9 4.9 %fusion.1 = f32[1,1,4,1024,1024]{4,3,2,1,0:T(8,128)} fusion(f32[1,1,4,1024,1024]{4,3,2,1,0:T(8,128)} %fusion.15, f32[4,1024,1024]{2,1,0:T(8,128)} %broadcast_multiply_fusion, f32[1024]{0:T(1024)S(1)} %broadcast_multiply_fusion.1), kind=kLoop, calls=%fused_computation.5 | loop fusion | flops 3145728 | bytes 8392704 | tf_op jit(solution)/shard_map/scatter-add | solution.py:51
  (8 shorter events, 0.2 us)
Async XLA Ops:
  0.6 1.0 copy-start
  3.8 13.2 %all-to-all-start = ((bf16[4,64,1024]{2,1,0:T(8,128)(2,1)}), bf16[4,64,1024]{2,1,0:T(8,128)(2,1)S(1)}, u32[]{:S(2)}, u32[]{:S(2)}) async-start(bf16[4,64,1024]{2,1,0:T(8,128)(2,1)} %copy.11), calls=%async_computation | async-start | bytes 1048576 | tf_op jit(solution)/shard_map/all_to_all | solution.py:27
  17.1 8.7 %collective-permute-start = (bf16[256,1024]{1,0:T(8,128)(2,1)S(1)}, bf16[256,1024]{1,0:T(8,128)(2,1)S(1)}, u32[]{:S(2)}, u32[]{:S(2)}) collective-permute-start(bf16[256,1024]{1,0:T(8,128)(2,1)S(1)} %copy.19), channel_id=1, source_target_pairs={{1,0},{2,1},{3,2},{4,3},{5,4},{6,5},{7,6},{0,7},{9,8},{10,9},{11,1... | collective-permute-start | bytes 1572872 | tf_op jit(solution)/shard_map/while/body/eval_jaxpr/ppermute | solution.py:10
  25.8 10.5 %collective-permute-start = (bf16[256,1024]{1,0:T(8,128)(2,1)S(1)}, bf16[256,1024]{1,0:T(8,128)(2,1)S(1)}, u32[]{:S(2)}, u32[]{:S(2)}) collective-permute-start(bf16[256,1024]{1,0:T(8,128)(2,1)S(1)} %copy.19), channel_id=1, source_target_pairs={{1,0},{2,1},{3,2},{4,3},{5,4},{6,5},{7,6},{0,7},{9,8},{10,9},{11,1... | collective-permute-start | bytes 1572872 | tf_op jit(solution)/shard_map/while/body/eval_jaxpr/ppermute | solution.py:10
  36.3 10.5 %collective-permute-start = (bf16[256,1024]{1,0:T(8,128)(2,1)S(1)}, bf16[256,1024]{1,0:T(8,128)(2,1)S(1)}, u32[]{:S(2)}, u32[]{:S(2)}) collective-permute-start(bf16[256,1024]{1,0:T(8,128)(2,1)S(1)} %copy.19), channel_id=1, source_target_pairs={{1,0},{2,1},{3,2},{4,3},{5,4},{6,5},{7,6},{0,7},{9,8},{10,9},{11,1... | collective-permute-start | bytes 1572872 | tf_op jit(solution)/shard_map/while/body/eval_jaxpr/ppermute | solution.py:10
  46.8 10.5 %collective-permute-start = (bf16[256,1024]{1,0:T(8,128)(2,1)S(1)}, bf16[256,1024]{1,0:T(8,128)(2,1)S(1)}, u32[]{:S(2)}, u32[]{:S(2)}) collective-permute-start(bf16[256,1024]{1,0:T(8,128)(2,1)S(1)} %copy.19), channel_id=1, source_target_pairs={{1,0},{2,1},{3,2},{4,3},{5,4},{6,5},{7,6},{0,7},{9,8},{10,9},{11,1... | collective-permute-start | bytes 1572872 | tf_op jit(solution)/shard_map/while/body/eval_jaxpr/ppermute | solution.py:10
where the time goes:
time: 131 us; the launch traced here: 130 us
  other arithmetic  30.1 us (23%)
  local copies, waits for them, and re-layouts  24.2 us (18%)
  waiting for transfers between devices  22 us (17%)
  starting transfers between devices  18.5 us (14%)
  blocking collectives  18 us (14%)
  matrix products  15.1 us (12%)
  between operations  2.03 us (2%)
    psum x1, blocking collectives, shards(): mu = lax.psum(local_trace, 'feat') / (width * lax.axis_size('feat'))  18 us
    gather x1, local copies, waits for them, and re-layouts, shards(): local_trace = jnp.sum(jnp.diagonal(grams[0]) / tokens)  17.3 us
    ppermute x4, waiting for transfers between devices, shifted(): return lax.ppermute(block, axis, route)  15.7 us
    ppermute x4, starting transfers between devices, shifted(): return lax.ppermute(block, axis, route)  13.3 us
    dot_general x5, matrix products, product(): lax.dot_general(left, right, (((0,), (0,)), ((), ())), preferred_element_...  12.8 us
    broadcast_in_dim x1, other arithmetic, shards(): return (factor[None, None], far[None, None])  12.4 us
    mul x1, other arithmetic, shards(): scaled = grams / tokens * (1.0 - weight)  12.2 us
    all_to_all x1, waiting for transfers between devices, shards(): lax.all_to_all(ordered, 'layer', split_axis=0, concat_axis=1, tiled=True)  6.21 us
  transfers between devices with their start and end apart: 5, of which 5 were waited for; matrix products, arithmetic and copies ran while one was open for 9% of the time, Pallas kernels for 0%

commit v1 on v0

--- a/solution.py
+++ b/solution.py
@@ -2,6 +2,18 @@
 import jax.numpy as jnp
 from jax import lax
 from jax.sharding import PartitionSpec as P
+
+
+def cut_along(value, dim, size):
+    dims = value.shape
+    blocks = value.reshape(*dims[:dim], size, dims[dim] // size, *dims[dim + 1 :])
+    return jnp.moveaxis(blocks, dim, 0)
+
+
+def in_order(blocks, dim):
+    dims = list(blocks.shape[1:])
+    dims[dim] *= blocks.shape[0]
+    return jnp.moveaxis(blocks, 0, dim).reshape(dims)
 
 
 def shifted(block, axis, distance):
@@ -24,7 +36,14 @@
     ordered = jnp.einsum("ds,stc->dtc", pick, acts, preferred_element_type=jnp.float32).astype(
         jnp.bfloat16
     )
-    gathered = lax.all_to_all(ordered, "layer", split_axis=0, concat_axis=1, tiled=True)
+    count, index_2 = (lax.axis_size("layer"), lax.axis_index("layer"))
+    blocks = cut_along(ordered, 0, count)
+    outs = [blocks[index_2]]
+    for lap in range(1, count):
+        sent = blocks[index_2 ^ lap]
+        outs.append(lax.ppermute(sent, "layer", [(i_2, i_2 ^ lap) for i_2 in range(count)]))
+    blocks = jnp.stack(outs)[index_2 ^ jnp.arange(count)]
+    gathered = in_order(blocks, 1)
     panel = gathered[0]
     tokens = panel.shape[0]
     width = panel.shape[1]

time: 131 us -> 136 us (1.038)
  waiting for transfers between devices: 22 us -> 25.3 us
    ppermute x0 -> x3, waiting for transfers between devices: none -> 9.58 us  [shards(): lax.ppermute(sent, 'layer', [(i_2, i_2 ^ lap) for i_2 in range(count)])]
    all_to_all x1 -> x0, waiting for transfers between devices: 6.21 us -> none  [shards(): lax.all_to_all(ordered, 'layer', split_axis=0, concat_axis=1, tiled=True)]
    all_to_all x1 -> x0, starting transfers between devices: 5.19 us -> none  [shards(): lax.all_to_all(ordered, 'layer', split_axis=0, concat_axis=1, tiled=True)]
    ppermute x0 -> x3, starting transfers between devices: none -> 4.63 us  [shards(): lax.ppermute(sent, 'layer', [(i_2, i_2 ^ lap) for i_2 in range(count)])]
  transfers between devices with their start and end apart: 5 -> 7, of which waited for: 5 -> 7; matrix products, arithmetic and copies ran while one was open for 9% -> 9% of each run, Pallas kernels for 0% -> 0%
where the time goes in v1:
time: 136 us; the launch traced here: 135 us
  other arithmetic  30.2 us (22%)
  waiting for transfers between devices  25.3 us (19%)
  local copies, waits for them, and re-layouts  24.9 us (18%)
  starting transfers between devices  19.1 us (14%)
  blocking collectives  17.9 us (13%)
  matrix products  15.1 us (11%)
  between operations  2.06 us (2%)
    psum x1, blocking collectives, shards(): mu = lax.psum(local_trace, 'feat') / (width * lax.axis_size('feat'))  17.9 us
    gather x1, local copies, waits for them, and re-layouts, shards(): local_trace = jnp.sum(jnp.diagonal(grams[0]) / tokens)  17.2 us
    ppermute x4, waiting for transfers between devices, shifted(): return lax.ppermute(block, axis, route)  15.8 us
    ppermute x4, starting transfers between devices, shifted(): return lax.ppermute(block, axis, route)  14.5 us
    dot_general x5, matrix products, product(): lax.dot_general(left, right, (((0,), (0,)), ((), ())), preferred_element_...  12.8 us
    broadcast_in_dim x1, other arithmetic, shards(): return (factor[None, None], far[None, None])  12.4 us
    mul x1, other arithmetic, shards(): scaled = grams / tokens * (1.0 - weight)  12.2 us
    ppermute x3, waiting for transfers between devices, shards(): lax.ppermute(sent, 'layer', [(i_2, i_2 ^ lap) for i_2 in range(count)])  9.58 us
  transfers between devices with their start and end apart: 7, of which 7 were waited for; matrix products, arithmetic and copies ran while one was open for 9% of the time, Pallas kernels for 0%

profile of v1, /device:TPU:0, one launch (start us, length us, event | category | flops | bytes accessed | tf_op | source)
XLA Modules:
  0.0 134.7 jit_solution(7669133510082230624)
XLA Ops:
  0.6 0.0 copy-start
  0.7 1.0 copy-done
  1.7 1.1 convolution_convert_fusion
  2.8 1.1 constant_dynamic-slice_fusion.3
  3.9 4.0 %collective-permute-start.3 = (bf16[1,64,1024]{2,0,1:T(2,128)(2,1)S(1)}, bf16[1,64,1024]{2,0,1:T(2,128)(2,1)S(1)}, u32[]{:S(2)}, u32[]{:S(2)}) collective-permute-start(bf16[1,64,1024]{2,0,1:T(2,128)(2,1)S(1)} %get-tuple-element.105), channel_id=1, source_target_pairs={{0,24},{8,16},{16,8},{24,0},{1,25},{9,17},{17,9},{25,1},{2,26},{10... | collective-permute-start | bytes 393224 | tf_op jit(solution)/shard_map/ppermute | solution.py:44
  7.9 0.5 collective-permute-start.2
  8.4 0.1 collective-permute-start.1
  8.6 1.1 fusion.5
  10.5 4.7 %collective-permute-done.3 = bf16[1,64,1024]{2,0,1:T(2,128)(2,1)S(1)} collective-permute-done((bf16[1,64,1024]{2,0,1:T(2,128)(2,1)S(1)}, bf16[1,64,1024]{2,0,1:T(2,128)(2,1)S(1)}, u32[]{:S(2)}, u32[]{:S(2)}) %collective-permute-start.3) | collective-permute-done | bytes 131104 | tf_op jit(solution)/shard_map/ppermute | solution.py:44
  15.2 4.7 %collective-permute-done.2 = bf16[1,64,1024]{2,0,1:T(2,128)(2,1)S(1)} collective-permute-done((bf16[1,64,1024]{2,0,1:T(2,128)(2,1)S(1)}, bf16[1,64,1024]{2,0,1:T(2,128)(2,1)S(1)}, u32[]{:S(2)}, u32[]{:S(2)}) %collective-permute-start.2) | collective-permute-done | bytes 131104 | tf_op jit(solution)/shard_map/ppermute | solution.py:44
  19.9 0.2 collective-permute-done.1
  20.2 0.1 maximum_bitcast_fusion
  20.3 0.6 gather_fusion
  20.9 41.5 %while.16 = (s32[]{:T(128)}, bf16[256,1024]{1,0:T(8,128)(2,1)S(1)}, f32[4,1024,1024]{2,1,0:T(8,128)}, bf16[256,1024]{1,0:T(8,128)(2,1)S(1)}, s32[]{:T(128)}) while((s32[]{:T(128)}, bf16[256,1024]{1,0:T(8,128)(2,1)S(1)}, f32[4,1024,1024]{2,1,0:T(8,128)}, bf16[256,1024]{1,0:T(8,128)(2,1)S(1)}, s32[]{:T(128)}) %tuple.42), condition=%wide.region_1.0_spmd, body=%wide.region_0.0_spmd.sunk | while | flops 536870912 | bytes 8388721 | solution.py:59
  20.9 3.2 %collective-permute-start = (bf16[256,1024]{1,0:T(8,128)(2,1)S(1)}, bf16[256,1024]{1,0:T(8,128)(2,1)S(1)}, u32[]{:S(2)}, u32[]{:S(2)}) collective-permute-start(bf16[256,1024]{1,0:T(8,128)(2,1)S(1)} %copy.33), channel_id=1, source_target_pairs={{1,0},{2,1},{3,2},{4,3},{5,4},{6,5},{7,6},{0,7},{9,8},{10,9},{11,1... | collective-permute-start | bytes 1572872 | tf_op jit(solution)/shard_map/while/body/eval_jaxpr/ppermute | solution.py:22
  24.2 2.8 %bitcast_dynamic-update-slice_fusion.2 = f32[4,1024,1024]{2,1,0:T(8,128)} fusion(f32[4,1024,1024]{2,1,0:T(8,128)} %get-tuple-element.140, s32[]{:T(128)S(6)} %copy.32, bf16[256,1024]{1,0:T(8,128)(2,1)S(1)} %get-tuple-element.146, bf16[256,1024]{1,0:T(8,128)(2,1)S(1)} %copy.33), kind=kOutput, calls=%fused_computation.2.clone.1 | convolution fusion | flops 536870912 | bytes 5242884 | tf_op jit(solution)/shard_map/while/body/eval_jaxpr/dot_general | solution.py:26
  26.9 3.9 %collective-permute-done = bf16[256,1024]{1,0:T(8,128)(2,1)S(1)} collective-permute-done((bf16[256,1024]{1,0:T(8,128)(2,1)S(1)}, bf16[256,1024]{1,0:T(8,128)(2,1)S(1)}, u32[]{:S(2)}, u32[]{:S(2)}) %collective-permute-start) | collective-permute-done | bytes 524320 | tf_op jit(solution)/shard_map/while/body/eval_jaxpr/ppermute | solution.py:22
  30.9 3.8 %collective-permute-start = (bf16[256,1024]{1,0:T(8,128)(2,1)S(1)}, bf16[256,1024]{1,0:T(8,128)(2,1)S(1)}, u32[]{:S(2)}, u32[]{:S(2)}) collective-permute-start(bf16[256,1024]{1,0:T(8,128)(2,1)S(1)} %copy.33), channel_id=1, source_target_pairs={{1,0},{2,1},{3,2},{4,3},{5,4},{6,5},{7,6},{0,7},{9,8},{10,9},{11,1... | collective-permute-start | bytes 1572872 | tf_op jit(solution)/shard_map/while/body/eval_jaxpr/ppermute | solution.py:22
  34.7 2.8 %bitcast_dynamic-update-slice_fusion.2 = f32[4,1024,1024]{2,1,0:T(8,128)} fusion(f32[4,1024,1024]{2,1,0:T(8,128)} %get-tuple-element.140, s32[]{:T(128)S(6)} %copy.32, bf16[256,1024]{1,0:T(8,128)(2,1)S(1)} %get-tuple-element.146, bf16[256,1024]{1,0:T(8,128)(2,1)S(1)} %copy.33), kind=kOutput, calls=%fused_computation.2.clone.1 | convolution fusion | flops 536870912 | bytes 5242884 | tf_op jit(solution)/shard_map/while/body/eval_jaxpr/dot_general | solution.py:26
  37.4 3.9 %collective-permute-done = bf16[256,1024]{1,0:T(8,128)(2,1)S(1)} collective-permute-done((bf16[256,1024]{1,0:T(8,128)(2,1)S(1)}, bf16[256,1024]{1,0:T(8,128)(2,1)S(1)}, u32[]{:S(2)}, u32[]{:S(2)}) %collective-permute-start) | collective-permute-done | bytes 524320 | tf_op jit(solution)/shard_map/while/body/eval_jaxpr/ppermute | solution.py:22
  41.4 3.8 %collective-permute-start = (bf16[256,1024]{1,0:T(8,128)(2,1)S(1)}, bf16[256,1024]{1,0:T(8,128)(2,1)S(1)}, u32[]{:S(2)}, u32[]{:S(2)}) collective-permute-start(bf16[256,1024]{1,0:T(8,128)(2,1)S(1)} %copy.33), channel_id=1, source_target_pairs={{1,0},{2,1},{3,2},{4,3},{5,4},{6,5},{7,6},{0,7},{9,8},{10,9},{11,1... | collective-permute-start | bytes 1572872 | tf_op jit(solution)/shard_map/while/body/eval_jaxpr/ppermute | solution.py:22
  45.2 2.8 %bitcast_dynamic-update-slice_fusion.2 = f32[4,1024,1024]{2,1,0:T(8,128)} fusion(f32[4,1024,1024]{2,1,0:T(8,128)} %get-tuple-element.140, s32[]{:T(128)S(6)} %copy.32, bf16[256,1024]{1,0:T(8,128)(2,1)S(1)} %get-tuple-element.146, bf16[256,1024]{1,0:T(8,128)(2,1)S(1)} %copy.33), kind=kOutput, calls=%fused_computation.2.clone.1 | convolution fusion | flops 536870912 | bytes 5242884 | tf_op jit(solution)/shard_map/while/body/eval_jaxpr/dot_general | solution.py:26
  47.9 3.9 %collective-permute-done = bf16[256,1024]{1,0:T(8,128)(2,1)S(1)} collective-permute-done((bf16[256,1024]{1,0:T(8,128)(2,1)S(1)}, bf16[256,1024]{1,0:T(8,128)(2,1)S(1)}, u32[]{:S(2)}, u32[]{:S(2)}) %collective-permute-start) | collective-permute-done | bytes 524320 | tf_op jit(solution)/shard_map/while/body/eval_jaxpr/ppermute | solution.py:22
  51.9 3.8 %collective-permute-start = (bf16[256,1024]{1,0:T(8,128)(2,1)S(1)}, bf16[256,1024]{1,0:T(8,128)(2,1)S(1)}, u32[]{:S(2)}, u32[]{:S(2)}) collective-permute-start(bf16[256,1024]{1,0:T(8,128)(2,1)S(1)} %copy.33), channel_id=1, source_target_pairs={{1,0},{2,1},{3,2},{4,3},{5,4},{6,5},{7,6},{0,7},{9,8},{10,9},{11,1... | collective-permute-start | bytes 1572872 | tf_op jit(solution)/shard_map/while/body/eval_jaxpr/ppermute | solution.py:22
  55.7 2.8 %bitcast_dynamic-update-slice_fusion.2 = f32[4,1024,1024]{2,1,0:T(8,128)} fusion(f32[4,1024,1024]{2,1,0:T(8,128)} %get-tuple-element.140, s32[]{:T(128)S(6)} %copy.32, bf16[256,1024]{1,0:T(8,128)(2,1)S(1)} %get-tuple-element.146, bf16[256,1024]{1,0:T(8,128)(2,1)S(1)} %copy.33), kind=kOutput, calls=%fused_computation.2.clone.1 | convolution fusion | flops 536870912 | bytes 5242884 | tf_op jit(solution)/shard_map/while/body/eval_jaxpr/dot_general | solution.py:26
  58.4 3.9 %collective-permute-done = bf16[256,1024]{1,0:T(8,128)(2,1)S(1)} collective-permute-done((bf16[256,1024]{1,0:T(8,128)(2,1)S(1)}, bf16[256,1024]{1,0:T(8,128)(2,1)S(1)}, u32[]{:S(2)}, u32[]{:S(2)}) %collective-permute-start) | collective-permute-done | bytes 524320 | tf_op jit(solution)/shard_map/while/body/eval_jaxpr/ppermute | solution.py:22
  62.4 4.7 %slice_bitcast_fusion = f32[1024,1024]{1,0:T(8,128)} fusion(f32[4,1024,1024]{2,1,0:T(8,128)} %get-tuple-element.94), kind=kLoop, calls=%fused_computation.7 | loop fusion | bytes 8388608 | tf_op jit(solution)/shard_map/squeeze | solution.py:62
  67.1 17.2 %gather_fusion.1 = f32[1024]{0:T(1024)S(1)} fusion(f32[1024,1024]{1,0:T(8,128)} %slice_bitcast_fusion, s32[1024]{0:T(1024)S(1)} %bitcast.52), kind=kCustom, calls=%fused_computation.1 | custom fusion | bytes 16384 | tf_op jit(solution)/shard_map/jit(diagonal)/cond/branch_0_fun/gather | solution.py:62
  84.2 0.6 multiply_reduce_fusion
  84.8 12.2 %broadcast_multiply_fusion = f32[4,1024,1024]{2,1,0:T(8,128)} fusion(f32[4,1024,1024]{2,1,0:T(8,128)} %get-tuple-element.94, f32[]{:T(128)S(6)} %mul.31), kind=kLoop, calls=%fused_computation.3 | loop fusion | flops 4194304 | bytes 33554436 | tf_op jit(solution)/shard_map/mul | solution.py:61
  97.0 12.4 %fusion.16 = f32[1,1,4,1024,1024]{4,3,2,1,0:T(8,128)} fusion(f32[4,1024,1024]{2,1,0:T(8,128)} %get-tuple-element.94, f32[]{:T(128)S(6)} %mul.31), kind=kLoop, calls=%fused_computation.39 | loop fusion | flops 4194304 | bytes 33554436 | tf_op jit(solution)/shard_map/broadcast_in_dim | solution.py:76
  109.4 17.9 %psum.7 = f32[]{:T(128)} all-reduce(f32[]{:T(128)} %multiply_reduce_fusion), channel_id=1, replica_groups=mesh['layer'=4,'feat'=8] {'feat'}, use_global_device_ids=true, to_apply=%region_3.4 | all-reduce | flops 1 | bytes 8 | tf_op jit(solution)/shard_map/psum | solution.py:63
  127.4 1.8 %multiply_bitcast_fusion = f32[1,1,512,1024]{3,2,1,0:T(8,128)} fusion(f32[]{:T(128)S(6)} %mul.31, bf16[256,1024]{1,0:T(8,128)(2,1)S(1)} %get-tuple-element.95, bf16[256,1024]{1,0:T(8,128)(2,1)S(1)} %get-tuple-element.148, pred[]{:T(512)S(6)} %lt.44), kind=kOutput, calls=%fused_computation.9 | convolution fusion | flops 269352960 | bytes 3671552 | tf_op jit(solution)/shard_map/dot_general | solution.py:26
  129.8 4.9 %fusion.1 = f32[1,1,4,1024,1024]{4,3,2,1,0:T(8,128)} fusion(f32[1,1,4,1024,1024]{4,3,2,1,0:T(8,128)} %fusion.16, f32[4,1024,1024]{2,1,0:T(8,128)} %broadcast_multiply_fusion, f32[1024]{0:T(1024)S(1)} %broadcast_multiply_fusion.1), kind=kLoop, calls=%fused_computation.6 | loop fusion | flops 3145728 | bytes 8392704 | tf_op jit(solution)/shard_map/scatter-add | solution.py:70
  (14 shorter events, 0.4 us)
Async XLA Ops:
  0.6 1.0 copy-start
  3.9 11.2 %collective-permute-start.3 = (bf16[1,64,1024]{2,0,1:T(2,128)(2,1)S(1)}, bf16[1,64,1024]{2,0,1:T(2,128)(2,1)S(1)}, u32[]{:S(2)}, u32[]{:S(2)}) collective-permute-start(bf16[1,64,1024]{2,0,1:T(2,128)(2,1)S(1)} %get-tuple-element.105), channel_id=1, source_target_pairs={{0,24},{8,16},{16,8},{24,0},{1,25},{9,17},{17,9},{25,1},{2,26},{10... | collective-permute-start | bytes 393224 | tf_op jit(solution)/shard_map/ppermute | solution.py:44
  7.9 11.9 %collective-permute-start.2 = (bf16[1,64,1024]{2,0,1:T(2,128)(2,1)S(1)}, bf16[1,64,1024]{2,0,1:T(2,128)(2,1)S(1)}, u32[]{:S(2)}, u32[]{:S(2)}) collective-permute-start(bf16[1,64,1024]{2,0,1:T(2,128)(2,1)S(1)} %get-tuple-element.106), channel_id=1, source_target_pairs={{0,16},{8,24},{16,0},{24,8},{1,17},{9,25},{17,1},{25,9},{2,18},{10... | collective-permute-start | bytes 393224 | tf_op jit(solution)/shard_map/ppermute | solution.py:44
  8.4 11.7 %collective-permute-start.1 = (bf16[1,64,1024]{2,0,1:T(2,128)(2,1)S(1)}, bf16[1,64,1024]{2,0,1:T(2,128)(2,1)S(1)}, u32[]{:S(2)}, u32[]{:S(2)}) collective-permute-start(bf16[1,64,1024]{2,0,1:T(2,128)(2,1)S(1)} %get-tuple-element.107), channel_id=1, source_target_pairs={{0,8},{8,0},{16,24},{24,16},{1,9},{9,1},{17,25},{25,17},{2,10},{10... | collective-permute-start | bytes 393224 | tf_op jit(solution)/shard_map/ppermute | solution.py:44
  20.9 9.9 %collective-permute-start = (bf16[256,1024]{1,0:T(8,128)(2,1)S(1)}, bf16[256,1024]{1,0:T(8,128)(2,1)S(1)}, u32[]{:S(2)}, u32[]{:S(2)}) collective-permute-start(bf16[256,1024]{1,0:T(8,128)(2,1)S(1)} %copy.33), channel_id=1, source_target_pairs={{1,0},{2,1},{3,2},{4,3},{5,4},{6,5},{7,6},{0,7},{9,8},{10,9},{11,1... | collective-permute-start | bytes 1572872 | tf_op jit(solution)/shard_map/while/body/eval_jaxpr/ppermute | solution.py:22
  30.9 10.5 %collective-permute-start = (bf16[256,1024]{1,0:T(8,128)(2,1)S(1)}, bf16[256,1024]{1,0:T(8,128)(2,1)S(1)}, u32[]{:S(2)}, u32[]{:S(2)}) collective-permute-start(bf16[256,1024]{1,0:T(8,128)(2,1)S(1)} %copy.33), channel_id=1, source_target_pairs={{1,0},{2,1},{3,2},{4,3},{5,4},{6,5},{7,6},{0,7},{9,8},{10,9},{11,1... | collective-permute-start | bytes 1572872 | tf_op jit(solution)/shard_map/while/body/eval_jaxpr/ppermute | solution.py:22
  41.4 10.5 %collective-permute-start = (bf16[256,1024]{1,0:T(8,128)(2,1)S(1)}, bf16[256,1024]{1,0:T(8,128)(2,1)S(1)}, u32[]{:S(2)}, u32[]{:S(2)}) collective-permute-start(bf16[256,1024]{1,0:T(8,128)(2,1)S(1)} %copy.33), channel_id=1, source_target_pairs={{1,0},{2,1},{3,2},{4,3},{5,4},{6,5},{7,6},{0,7},{9,8},{10,9},{11,1... | collective-permute-start | bytes 1572872 | tf_op jit(solution)/shard_map/while/body/eval_jaxpr/ppermute | solution.py:22
  51.9 10.5 %collective-permute-start = (bf16[256,1024]{1,0:T(8,128)(2,1)S(1)}, bf16[256,1024]{1,0:T(8,128)(2,1)S(1)}, u32[]{:S(2)}, u32[]{:S(2)}) collective-permute-start(bf16[256,1024]{1,0:T(8,128)(2,1)S(1)} %copy.33), channel_id=1, source_target_pairs={{1,0},{2,1},{3,2},{4,3},{5,4},{6,5},{7,6},{0,7},{9,8},{10,9},{11,1... | collective-permute-start | bytes 1572872 | tf_op jit(solution)/shard_map/while/body/eval_jaxpr/ppermute | solution.py:22
